TPU v7x, 256 devices: a whole 4x4x8 slice. The times are simulated.
256 devices in a mesh: expert: 128 (over x, z, y), dp: 2 (over core).
Axes of the slice: x: 4, y: 4, z: 8, core: 2. Of those that a mesh axis runs over, the one named last changes fastest.
Arguments:
- tokens: bfloat16 [16384, 4096], P(('expert', 'dp')), may hold values from -6 to 6
- routes: int32 [16384, 8], P(('expert', 'dp')), may hold values from 0 to 127, all different within a row; in each aligned block of 64 rows (0 to 63, 64 to 127, ...) at most 8 rows name the same one
- gate_probs: float32 [16384, 8], P(('expert', 'dp')), may hold values from 0.05 to 0.35
- gate_w: bfloat16 [128, 4096, 768], P('expert', None, 'dp'), may hold values from -0.09375 to 0.09375
- up_w: bfloat16 [128, 4096, 768], P('expert', None, 'dp'), may hold values from -0.09375 to 0.09375
- down_w: bfloat16 [128, 768, 4096], P('expert', 'dp'), may hold values from -0.21875 to 0.21875
Outputs:
- mixed_out: bfloat16 [16384, 4096], P(('expert', 'dp'))
Inputs may be any that keep to these rules, and one draw needn't show every extreme that they name: `routes`: each token names 8 different experts. Among the 64 tokens of one device (aligned blocks of rows), no expert is named by more than 8 tokens; in some block an expert is named by exactly 8 tokens.
All inputs are finite; a program needn't handle non-finite values.
Results may differ from a plain program's by a relative error of at most 0.0057.
Values may be sent and summed in bfloat16 or wider, within the bound.
No kernel may reach another device: no remote copies, remote signals or barrier semaphores. Data moves between devices by JAX's collectives and lax.ppermute only.
A program may use at most 192 MiB of HBM per device.

v0:
```python
import jax
import jax.numpy as jnp
from jax import lax
from jax.sharding import PartitionSpec as P


def swiglu(row_block, w_gate, w_up, w_down):
    gate_act = jnp.dot(row_block, w_gate, preferred_element_type=jnp.float32)
    up_act = jnp.dot(row_block, w_up, preferred_element_type=jnp.float32)
    hidden = (jax.nn.silu(gate_act) * up_act).astype(jnp.bfloat16)
    return jnp.dot(hidden, w_down, preferred_element_type=jnp.float32)


def apply_expert(row_block, w_gate, w_up, w_down):
    return swiglu(row_block, w_gate, w_up, w_down)


def body(tokens, routes, gate_probs, gate_w, up_w, down_w):
    experts = lax.axis_size("expert")
    tok_count, model_width = tokens.shape
    top_count = routes.shape[1]
    capacity = 2 * tok_count * top_count // experts
    expert_ids = jnp.arange(experts, dtype=jnp.int32)
    named_hits = jnp.sum((routes[:, :, None] == expert_ids).astype(jnp.int32), axis=1)
    before = jnp.cumsum(named_hits, axis=0) - named_hits
    slot_index = jnp.take_along_axis(before, routes, axis=1)
    target = routes * capacity + slot_index
    buffer_rows = jnp.arange(experts * capacity, dtype=jnp.int32)
    placer = jnp.sum(
        (target[None, :, :] == buffer_rows[:, None, None]).astype(jnp.float32), axis=2
    ).astype(jnp.bfloat16)
    outgoing = jnp.dot(placer, tokens, preferred_element_type=jnp.float32).astype(jnp.bfloat16)
    outgoing = outgoing.reshape(experts, capacity, model_width)
    present = (
        jnp.sum(placer.astype(jnp.float32), axis=1).astype(jnp.bfloat16).reshape(experts, capacity)
    )
    w_gate = gate_w[0]
    w_up = up_w[0]
    w_down = down_w[0]
    row_block = lax.all_to_all(outgoing, "expert", split_axis=0, concat_axis=0, tiled=True)
    flag_block = lax.all_to_all(present, "expert", split_axis=0, concat_axis=0, tiled=True)
    source_count = row_block.shape[0]
    item_count = row_block.shape[1]
    flat_rows = row_block.reshape(-1, model_width)
    flat_flags = flag_block.reshape(-1)
    both_rows = lax.all_gather(flat_rows, "dp", axis=0, tiled=True)
    partial_out = apply_expert(both_rows, w_gate, w_up, w_down)
    result = lax.psum_scatter(partial_out, "dp", scatter_dimension=0, tiled=True)
    masked = result * flat_flags.astype(jnp.float32)[:, None]
    answered = masked.astype(jnp.bfloat16).reshape(source_count, item_count, model_width)
    returned = lax.all_to_all(answered, "expert", split_axis=0, concat_axis=0, tiled=True)
    picked = returned.reshape(experts * capacity, model_width)[target]
    mixed_out = jnp.einsum(
        "tk,tkd->td", gate_probs, picked.astype(jnp.float32), precision=lax.Precision.HIGHEST
    )
    return mixed_out.astype(jnp.bfloat16)


def solution(mesh):
    return jax.shard_map(
        body,
        mesh=mesh,
        in_specs=(
            P(("expert", "dp"), None),
            P(("expert", "dp"), None),
            P(("expert", "dp"), None),
            P("expert", None, "dp"),
            P("expert", None, "dp"),
            P("expert", "dp", None),
        ),
        out_specs=P(("expert", "dp"), None),
        check_vma=False,
    )
```

profile of v0, /device:TPU:2, one launch (start us, length us, event | category | flops | bytes accessed | tf_op | source)
XLA Modules:
  0.0 579.9 jit_solution(941686837038767233)
XLA Ops:
  6.5 0.8 bitcast_or_fusion
  7.4 0.9 copy.35
  8.3 0.1 copy.36
  8.4 0.1 reshape.50
  8.4 0.1 convert_reduce_fusion.1
  8.6 0.1 reduce_window_sum.11
  8.7 3.6 gather_fusion.1
  12.3 0.1 reshape.53
  12.4 0.1 copy.37
  12.5 0.1 copy.38
  12.6 0.7 convert_reduce_fusion
  13.3 3.4 convert_bitcast_fusion
  16.7 201.5 %all_to_all.20 = bf16[128,8,4096]{2,1,0:T(8,128)(2,1)} all-to-all(bf16[128,8,4096]{2,1,0:T(8,128)(2,1)S(1)} %convert_bitcast_fusion), channel_id=1, replica_groups=mesh['expert'=128,'dp'=2] {'expert'}, dimensions={0} | all-to-all | bytes 16777216 | tf_op jit(solution)/shard_map/all_to_all | solution.py:40
  218.3 0.2 reduce-scatter.2.cloned.1.call-start
  218.5 31.1 %all-gather.2.cloned.1.call-done = bf16[2048,4096]{1,0:T(8,128)(2,1)} async-done(((bf16[1024,4096]{1,0:T(8,128)(2,1)}), bf16[2048,4096]{1,0:T(8,128)(2,1)}) %all-gather.2.cloned.1.call-update) | async-done | bytes 16777232 | tf_op jit(solution)/shard_map/all_gather | solution.py:46
  249.6 13.0 %fusion.6 = f32[2048,384]{1,0:T(8,128)S(1)} fusion(bf16[2048,4096]{1,0:T(8,128)(2,1)} %all-gather.2.cloned.1.call-done, bf16[1,4096,384]{2,1,0:T(8,128)(2,1)} %param.9), kind=kOutput, calls=%fused_computation.11 | convolution fusion | flops 6442450944 | bytes 23068672 | tf_op jit(solution)/shard_map/dot_general | solution.py:8
  262.6 12.5 %fusion.8 = bf16[2048,384]{1,0:T(8,128)(2,1)S(1)} fusion(bf16[2048,4096]{1,0:T(8,128)(2,1)} %all-gather.2.cloned.1.call-done, bf16[1,4096,384]{2,1,0:T(8,128)(2,1)S(1)} %copy-done.4, f32[2048,384]{1,0:T(8,128)S(1)} %fusion.6), kind=kOutput, calls=%fused_computation.13 | convolution fusion | flops 6447169536 | bytes 24641536 | tf_op jit(solution)/shard_map/dot_general | solution.py:9
  275.2 14.5 %fusion.3 = f32[2048,4096]{1,0:T(8,128)} fusion(bf16[2048,384]{1,0:T(8,128)(2,1)S(1)} %fusion.8, bf16[1,384,4096]{2,1,0:T(8,128)(2,1)S(1)} %copy-done), kind=kOutput, calls=%fused_computation.8 | convolution fusion | flops 6442450944 | bytes 38273024 | tf_op jit(solution)/shard_map/dot_general | solution.py:11
  289.7 0.1 all_to_all.16
  289.8 24.6 %all_to_all.21 = bf16[128,1,8]{2,1,0:T(2,128)(2,1)S(1)} all-to-all(bf16[128,1,8]{2,1,0:T(2,128)(2,1)S(1)} %all_to_all.16), channel_id=1, replica_groups=mesh['expert'=128,'dp'=2] {'expert'}, dimensions={0} | all-to-all | bytes 4096 | tf_op jit(solution)/shard_map/all_to_all | solution.py:41
  314.4 0.2 convert_reduce_fusion.2
  314.6 0.1 reshape.41
  314.7 27.0 %reduce-scatter.2.cloned.1.call-done = f32[1024,4096]{1,0:T(8,128)} async-done(((f32[2048,4096]{1,0:T(8,128)}), f32[1024,4096]{1,0:T(8,128)}) %reduce-scatter.2.cloned.1.call-update) | async-done | bytes 16777232 | tf_op jit(solution)/shard_map/reduce_scatter | solution.py:48
  341.6 9.3 %fusion = bf16[128,8,4096]{2,1,0:T(8,128)(2,1)} fusion(f32[1024,4096]{1,0:T(8,128)} %reduce-scatter.2.cloned.1.call-done, f32[1024]{0:T(1024)S(1)} %reshape.41), kind=kLoop, calls=%fused_computation.3 | loop fusion | flops 8388608 | bytes 25169920 | tf_op jit(solution)/shard_map/reshape | solution.py:50
  350.9 14.5 %all-to-all-start.2 = ((bf16[128,8,4096]{2,1,0:T(8,128)(2,1)}), bf16[128,8,4096]{2,1,0:T(8,128)(2,1)}, u32[]{:S(2)}, u32[]{:S(2)}) async-start(bf16[128,8,4096]{2,1,0:T(8,128)(2,1)} %fusion), calls=%async_computation.3 | async-start | bytes 16777216 | tf_op jit(solution)/shard_map/all_to_all | solution.py:51
  365.4 0.1 copy.41
  365.5 0.1 copy.40
  365.6 0.1 reshape.44
  365.7 187.1 %all-to-all-done.2 = bf16[128,8,4096]{2,1,0:T(8,128)(2,1)} async-done(((bf16[128,8,4096]{2,1,0:T(8,128)(2,1)}), bf16[128,8,4096]{2,1,0:T(8,128)(2,1)}, u32[]{:S(2)}, u32[]{:S(2)}) %all-to-all-start.2) | async-done | bytes 8388640 | tf_op jit(solution)/shard_map/all_to_all | solution.py:51
  552.8 13.2 %gather_fusion = bf16[512,4096]{1,0:T(8,128)(2,1)} fusion(bf16[1024,4096]{1,0:T(8,128)(2,1)} %bitcast.7, s32[1024]{0:T(1024)S(1)} %pad_clamp_fusion), kind=kCustom, calls=%fused_computation | custom fusion | bytes 8390656 | tf_op jit(solution)/shard_map/gather | solution.py:52
  565.9 5.7 fusion.1
  571.6 1.4 copy.44
  (17 shorter events, 0.1 us)
Async XLA Ops:
  6.5 268.6 %copy-start = (bf16[1,384,4096]{2,1,0:T(8,128)(2,1)S(1)}, bf16[1,384,4096]{2,1,0:T(8,128)(2,1)}, u32[]{:S(2)}) copy-start(bf16[1,384,4096]{2,1,0:T(8,128)(2,1)} %param.11) | copy-start | bytes 9437188
  6.5 243.1 %all-gather.2.cloned.1.call-start = ((), (), s32[]{:S(2)}) async-start(), calls=%async_computation.4 | async-start | bytes 25165824 | tf_op jit(solution)/shard_map/all_gather | solution.py:46
  8.7 3.8 copy-start.2
  218.3 123.3 %reduce-scatter.2.cloned.1.call-start = ((), (), s32[]{:S(2)}) async-start(), calls=%async_computation.5 | async-start | bytes 50331648 | tf_op jit(solution)/shard_map/reduce_scatter | solution.py:48
  249.6 13.0 %copy-start.4 = (bf16[1,4096,384]{2,1,0:T(8,128)(2,1)S(1)}, bf16[1,4096,384]{2,1,0:T(8,128)(2,1)}, u32[]{:S(2)}) copy-start(bf16[1,4096,384]{2,1,0:T(8,128)(2,1)} %param.10) | copy-start | bytes 9437188
  350.9 14.5 %copy-start.3 = (f32[64,8]{0,1:T(8,128)S(1)}, f32[64,8]{0,1:T(8,128)}, u32[]{:S(2)}) copy-start(f32[64,8]{0,1:T(8,128)} %param.8) | copy-start | bytes 6148
  350.9 201.8 %all-to-all-start.2 = ((bf16[128,8,4096]{2,1,0:T(8,128)(2,1)}), bf16[128,8,4096]{2,1,0:T(8,128)(2,1)}, u32[]{:S(2)}, u32[]{:S(2)}) async-start(bf16[128,8,4096]{2,1,0:T(8,128)(2,1)} %fusion), calls=%async_computation.3 | async-start | bytes 16777216 | tf_op jit(solution)/shard_map/all_to_all | solution.py:51
  552.8 20.3 %copy-start.1 = (bf16[1,384,4096]{2,1,0:T(8,128)(2,1)S(1)}, bf16[1,384,4096]{2,1,0:T(8,128)(2,1)}, u32[]{:S(2)}) copy-start(bf16[1,384,4096]{2,1,0:T(8,128)(2,1)} %param.11) | copy-start | bytes 9437188
Sparse Core Ops, SparseCore 0:
  218.4 31.1 all-gather.1
  289.8 51.7 reduce-scatter.1
where the time goes:
time: 580 us
  waiting for transfers between devices  245 us (42%)
  blocking collectives  226 us (39%)
  matrix products  49.1 us (8%)
  local copies, waits for them, and re-layouts  19.9 us (3%)
  starting transfers between devices  14.7 us (3%)
  between operations  13.5 us (2%)
  other arithmetic  11.3 us (2%)
    all_to_all x1, blocking collectives, body(): lax.all_to_all(outgoing, 'expert', split_axis=0, concat_axis=0, tiled=True)  202 us
    all_to_all x1, waiting for transfers between devices, body(): lax.all_to_all(answered, 'expert', split_axis=0, concat_axis=0, tiled=True)  187 us
    all_gather x1, waiting for transfers between devices, body(): both_rows = lax.all_gather(flat_rows, 'dp', axis=0, tiled=True)  31.1 us
    reduce_scatter x1, waiting for transfers between devices, body(): lax.psum_scatter(partial_out, 'dp', scatter_dimension=0, tiled=True)  27 us
    all_to_all x1, blocking collectives, body(): lax.all_to_all(present, 'expert', split_axis=0, concat_axis=0, tiled=True)  24.6 us
    dot_general x1, matrix products, swiglu(): return jnp.dot(hidden, w_down, preferred_element_type=jnp.float32)  14.5 us
    all_to_all x1, starting transfers between devices, body(): lax.all_to_all(answered, 'expert', split_axis=0, concat_axis=0, tiled=True)  14.5 us
    gather x1, local copies, waits for them, and re-layouts, body(): picked = returned.reshape(experts * capacity, model_width)[target]  13.2 us
  transfers between devices with their start and end apart: 3, of which 3 were waited for; matrix products, arithmetic and copies ran while one was open for 0% of the time, Pallas kernels for 0%

commit v1 on v0

--- a/solution.py
+++ b/solution.py
@@ -43,7 +43,10 @@
     item_count = row_block.shape[1]
     flat_rows = row_block.reshape(-1, model_width)
     flat_flags = flag_block.reshape(-1)
-    both_rows = lax.all_gather(flat_rows, "dp", axis=0, tiled=True)
+    devices = lax.axis_size("dp")
+    pieces = jnp.stack([flat_rows for _ in range(devices)])
+    pieces = lax.all_to_all(pieces, "dp", split_axis=0, concat_axis=0)
+    both_rows = jnp.concatenate(pieces, axis=0)
     partial_out = apply_expert(both_rows, w_gate, w_up, w_down)
     result = lax.psum_scatter(partial_out, "dp", scatter_dimension=0, tiled=True)
     masked = result * flat_flags.astype(jnp.float32)[:, None]

time: 580 us -> 564 us (0.972)
  waiting for transfers between devices: 245 us -> 214 us
  blocking collectives: 226 us -> 240 us
    all_gather x1 -> x0, waiting for transfers between devices: 31.1 us -> none  [body(): both_rows = lax.all_gather(flat_rows, 'dp', axis=0, tiled=True)]
    all_to_all x0 -> x1, blocking collectives: none -> 19.3 us  [body(): pieces = lax.all_to_all(pieces, 'dp', split_axis=0, concat_axis=0)]
  transfers between devices with their start and end apart: 3 -> 2, of which waited for: 3 -> 2; matrix products, arithmetic and copies ran while one was open for 0% -> 0% of each run, Pallas kernels for 0% -> 0%
where the time goes in v1:
time: 564 us
  blocking collectives  240 us (43%)
  waiting for transfers between devices  214 us (38%)
  matrix products  49.4 us (9%)
  local copies, waits for them, and re-layouts  19.9 us (4%)
  starting transfers between devices  14.5 us (3%)
  between operations  13.5 us (2%)
  other arithmetic  12.9 us (2%)
    all_to_all x1, blocking collectives, body(): lax.all_to_all(outgoing, 'expert', split_axis=0, concat_axis=0, tiled=True)  201 us
    all_to_all x1, waiting for transfers between devices, body(): lax.all_to_all(answered, 'expert', split_axis=0, concat_axis=0, tiled=True)  187 us
    reduce_scatter x1, waiting for transfers between devices, body(): lax.psum_scatter(partial_out, 'dp', scatter_dimension=0, tiled=True)  27 us
    all_to_all x1, blocking collectives, body(): pieces = lax.all_to_all(pieces, 'dp', split_axis=0, concat_axis=0)  19.3 us
    all_to_all x1, blocking collectives, body(): lax.all_to_all(present, 'expert', split_axis=0, concat_axis=0, tiled=True)  19 us
    dot_general x1, matrix products, swiglu(): gate_act = jnp.dot(row_block, w_gate, preferred_element_type=jnp.float32)  15.2 us
    dot_general x1, matrix products, swiglu(): return jnp.dot(hidden, w_down, preferred_element_type=jnp.float32)  14.5 us
    all_to_all x1, starting transfers between devices, body(): lax.all_to_all(answered, 'expert', split_axis=0, concat_axis=0, tiled=True)  14.5 us
  transfers between devices with their start and end apart: 2, of which 2 were waited for; matrix products, arithmetic and copies ran while one was open for 0% of the time, Pallas kernels for 0%

profile of v1, /device:TPU:2, one launch (start us, length us, event | category | flops | bytes accessed | tf_op | source)
XLA Modules:
  0.0 564.0 jit_solution(18133866929426200479)
XLA Ops:
  6.5 0.8 bitcast_or_fusion
  7.4 0.9 copy.35
  8.3 0.1 copy.36
  8.4 0.1 reshape.50
  8.4 0.1 convert_reduce_fusion.1
  8.6 0.1 reduce_window_sum.11
  8.7 3.6 gather_fusion.1
  12.3 0.1 reshape.53
  12.4 0.1 copy.37
  12.5 0.1 copy.38
  12.6 0.7 convert_reduce_fusion
  13.3 3.4 convert_bitcast_fusion
  16.7 201.4 %all_to_all.25 = bf16[128,8,4096]{2,1,0:T(8,128)(2,1)S(1)} all-to-all(bf16[128,8,4096]{2,1,0:T(8,128)(2,1)S(1)} %convert_bitcast_fusion), channel_id=1, replica_groups=mesh['expert'=128,'dp'=2] {'expert'}, dimensions={0} | all-to-all | bytes 16777216 | tf_op jit(solution)/shard_map/all_to_all | solution.py:40
  218.1 1.5 pad_maximum_fusion
  219.7 19.3 %all_to_all.26 = bf16[2,1024,4096]{2,1,0:T(8,128)(2,1)} all-to-all(bf16[2,1024,4096]{2,1,0:T(8,128)(2,1)S(1)} %pad_maximum_fusion), channel_id=1, replica_groups=mesh['expert'=128,'dp'=2] {'dp'}, dimensions={0} | all-to-all | bytes 33554432 | tf_op jit(solution)/shard_map/all_to_all | solution.py:48
  239.0 15.2 %fusion.6 = f32[2048,384]{1,0:T(8,128)} fusion(bf16[2048,4096]{1,0:T(8,128)(2,1)} %bitcast.36, bf16[1,4096,384]{2,1,0:T(8,128)(2,1)S(1)} %copy-done.5), kind=kOutput, calls=%fused_computation.12 | convolution fusion | flops 6442450944 | bytes 23068672 | tf_op jit(solution)/shard_map/dot_general | solution.py:8
  254.3 10.6 %fusion.8 = bf16[2048,384]{1,0:T(8,128)(2,1)S(1)} fusion(bf16[2048,4096]{1,0:T(8,128)(2,1)S(1)} %bitcast.37, bf16[1,4096,384]{2,1,0:T(8,128)(2,1)S(1)} %copy-done.6, f32[2048,384]{1,0:T(8,128)} %fusion.6), kind=kOutput, calls=%fused_computation.14 | convolution fusion | flops 6447169536 | bytes 24641536 | tf_op jit(solution)/shard_map/dot_general | solution.py:9
  264.9 14.5 %fusion.3 = f32[2048,4096]{1,0:T(8,128)} fusion(bf16[2048,384]{1,0:T(8,128)(2,1)S(1)} %fusion.8, bf16[1,384,4096]{2,1,0:T(8,128)(2,1)S(1)} %copy-done), kind=kOutput, calls=%fused_computation.9 | convolution fusion | flops 6442450944 | bytes 38273024 | tf_op jit(solution)/shard_map/dot_general | solution.py:11
  279.4 0.1 all_to_all.20
  279.5 19.0 %all_to_all.27 = bf16[128,1,8]{2,1,0:T(2,128)(2,1)S(1)} all-to-all(bf16[128,1,8]{2,1,0:T(2,128)(2,1)S(1)} %all_to_all.20), channel_id=1, replica_groups=mesh['expert'=128,'dp'=2] {'expert'}, dimensions={0} | all-to-all | bytes 4096 | tf_op jit(solution)/shard_map/all_to_all | solution.py:41
  298.5 0.2 convert_reduce_fusion.2
  298.7 0.1 reshape.41
  298.8 27.0 %reduce-scatter.2.cloned.1.call-done = f32[1024,4096]{1,0:T(8,128)} async-done(((f32[2048,4096]{1,0:T(8,128)}), f32[1024,4096]{1,0:T(8,128)}) %reduce-scatter.2.cloned.1.call-update) | async-done | bytes 16777232 | tf_op jit(solution)/shard_map/reduce_scatter | solution.py:51
  325.8 9.3 %fusion = bf16[128,8,4096]{2,1,0:T(8,128)(2,1)} fusion(f32[1024,4096]{1,0:T(8,128)} %reduce-scatter.2.cloned.1.call-done, f32[1024]{0:T(1024)S(1)} %reshape.41), kind=kLoop, calls=%fused_computation.4 | loop fusion | flops 8388608 | bytes 25169920 | tf_op jit(solution)/shard_map/reshape | solution.py:53
  335.1 14.5 %all-to-all-start.3 = ((bf16[128,8,4096]{2,1,0:T(8,128)(2,1)}), bf16[128,8,4096]{2,1,0:T(8,128)(2,1)}, u32[]{:S(2)}, u32[]{:S(2)}) async-start(bf16[128,8,4096]{2,1,0:T(8,128)(2,1)} %fusion), calls=%async_computation.4 | async-start | bytes 16777216 | tf_op jit(solution)/shard_map/all_to_all | solution.py:54
  349.6 0.1 copy.41
  349.7 0.1 copy.40
  349.8 0.1 reshape.44
  349.9 187.1 %all-to-all-done.3 = bf16[128,8,4096]{2,1,0:T(8,128)(2,1)} async-done(((bf16[128,8,4096]{2,1,0:T(8,128)(2,1)}), bf16[128,8,4096]{2,1,0:T(8,128)(2,1)}, u32[]{:S(2)}, u32[]{:S(2)}) %all-to-all-start.3) | async-done | bytes 8388640 | tf_op jit(solution)/shard_map/all_to_all | solution.py:54
  536.9 13.2 %gather_fusion = bf16[512,4096]{1,0:T(8,128)(2,1)} fusion(bf16[1024,4096]{1,0:T(8,128)(2,1)} %bitcast.8, s32[1024]{0:T(1024)S(1)} %pad_clamp_fusion), kind=kCustom, calls=%fused_computation | custom fusion | bytes 8390656 | tf_op jit(solution)/shard_map/gather | solution.py:55
  550.1 5.7 %fusion.1 = bf16[64,1,4096]{2,1,0:T(2,128)(2,1)S(1)} fusion(f32[64,8,1]{1,2,0:T(1,128)S(1)} %copy.41, bf16[512,4096]{1,0:T(8,128)(2,1)} %gather_fusion), kind=kOutput, calls=%fused_computation.6 | convolution fusion | flops 25165824 | bytes 4720640 | tf_op jit(solution)/shard_map/tk,tkd->td/dot_general | solution.py:56
  555.8 1.4 copy.44
  (20 shorter events, 0.1 us)
Async XLA Ops:
  6.5 258.3 %copy-start = (bf16[1,384,4096]{2,1,0:T(8,128)(2,1)S(1)}, bf16[1,384,4096]{2,1,0:T(8,128)(2,1)}, u32[]{:S(2)}) copy-start(bf16[1,384,4096]{2,1,0:T(8,128)(2,1)} %param.11) | copy-start | bytes 9437188
  6.5 319.3 %reduce-scatter.2.cloned.1.call-start = ((), (), s32[]{:S(2)}) async-start(), calls=%async_computation.5 | async-start | bytes 50331648 | tf_op jit(solution)/shard_map/reduce_scatter | solution.py:51
  8.7 3.8 copy-start.3
  219.7 19.3 %copy-start.5 = (bf16[1,4096,384]{2,1,0:T(8,128)(2,1)S(1)}, bf16[1,4096,384]{2,1,0:T(8,128)(2,1)}, u32[]{:S(2)}) copy-start(bf16[1,4096,384]{2,1,0:T(8,128)(2,1)} %param.9) | copy-start | bytes 9437188
  239.0 15.3 %copy-start.2 = (bf16[2,1024,4096]{2,1,0:T(8,128)(2,1)S(1)}, bf16[2,1024,4096]{2,1,0:T(8,128)(2,1)}, u32[]{:S(2)}) copy-start(bf16[2,1024,4096]{2,1,0:T(8,128)(2,1)} %all_to_all.26) | copy-start | bytes 50331652
  239.0 15.3 %copy-start.6 = (bf16[1,4096,384]{2,1,0:T(8,128)(2,1)S(1)}, bf16[1,4096,384]{2,1,0:T(8,128)(2,1)}, u32[]{:S(2)}) copy-start(bf16[1,4096,384]{2,1,0:T(8,128)(2,1)} %param.10) | copy-start | bytes 9437188
  335.1 14.5 %copy-start.4 = (f32[64,8]{0,1:T(8,128)S(1)}, f32[64,8]{0,1:T(8,128)}, u32[]{:S(2)}) copy-start(f32[64,8]{0,1:T(8,128)} %param.8) | copy-start | bytes 6148
  335.1 201.8 %all-to-all-start.3 = ((bf16[128,8,4096]{2,1,0:T(8,128)(2,1)}), bf16[128,8,4096]{2,1,0:T(8,128)(2,1)}, u32[]{:S(2)}, u32[]{:S(2)}) async-start(bf16[128,8,4096]{2,1,0:T(8,128)(2,1)} %fusion), calls=%async_computation.4 | async-start | bytes 16777216 | tf_op jit(solution)/shard_map/all_to_all | solution.py:54
  536.9 20.3 %copy-start.1 = (bf16[1,384,4096]{2,1,0:T(8,128)(2,1)S(1)}, bf16[1,384,4096]{2,1,0:T(8,128)(2,1)}, u32[]{:S(2)}) copy-start(bf16[1,384,4096]{2,1,0:T(8,128)(2,1)} %param.11) | copy-start | bytes 9437188
Sparse Core Ops, SparseCore 0:
  279.5 46.2 reduce-scatter.1
